TPU v7x, 32 devices: a whole 2x2x4 slice. The times are simulated.
32 devices in a mesh: orb: 16 (over z, x, core), aux: 2 (over y).
Axes of the slice: x: 2, y: 2, z: 4, core: 2. Of those that a mesh axis runs over, the one named last changes fastest.
Arguments:
- three_index: float32 [56, 1024, 2048], P(None, 'aux', 'orb'), may hold values from -0.5 to 0.5
- pair_density: float32 [3136, 3136], P('orb'), as said below
- active_orbitals: int32 [56], replicated, may hold values from 200 to 2047, as said below
- screen_mask: int32 [64, 128], P('aux', 'orb'), may hold values from 0 to 1
- one_density: float32 [56, 56], replicated
- inactive_fock: float32 [2048, 256], P('orb'), may hold values from -6 to 6
- active_fock: float32 [2048, 200], P('orb'), may hold values from -6 to 6
Outputs:
- rotation_gradient: float32 [2048, 256], P(('orb', 'aux'))
Inputs may be any that keep to these rules, and one draw needn't show every extreme that they name: `active_orbitals`: 56 distinct orbital indices. pair_density is symmetric: its entry at (tu, vw) equals that at (vw, tu).
All inputs are finite; a program needn't handle non-finite values.
Results may differ from a plain program's by a relative error of at most 0.0001.
Values sent between devices are 32-bit elements; how exact they have to be, the bound alone decides.
No kernel may reach another device: no remote copies, remote signals or barrier semaphores. Data moves between devices by JAX's collectives and lax.ppermute only.
A program may use at most 128 MiB of HBM per device.

v0:
```python
import jax
import jax.numpy as jnp
from jax import lax
from jax.sharding import PartitionSpec as P


def shards(
    three_index, pair_density, active_orbitals, screen_mask, one_density, inactive_fock, active_fock
):
    highest = lax.Precision.HIGHEST
    act_count = three_index.shape[0]
    slab_count = three_index.shape[1]
    row_count = three_index.shape[2]
    inactive_count = active_fock.shape[1]
    orb_position = lax.axis_index("orb")
    kept_mask = jnp.repeat(
        jnp.repeat(screen_mask.astype(jnp.float32), slab_count // screen_mask.shape[0], axis=0),
        row_count // screen_mask.shape[1],
        axis=1,
    )
    screened = three_index * kept_mask[None]
    global_rows = orb_position * row_count + jnp.arange(row_count, dtype=jnp.int32)
    active_pick = (global_rows[:, None] == active_orbitals[None, :]).astype(jnp.float32)
    partial_pairs = jnp.einsum("wPp,pv->Pvw", screened, active_pick, precision=highest).reshape(
        slab_count, act_count * act_count
    )
    pairs = lax.psum(partial_pairs, "orb")
    column_block = jnp.dot(pairs, pair_density.T, precision=highest)
    half = lax.all_gather(column_block, "orb", axis=1, tiled=True)
    q_partial = jnp.einsum(
        "uPp,Ptu->pt", screened, half.reshape(slab_count, act_count, act_count), precision=highest
    )
    occ_index = jnp.concatenate([jnp.arange(inactive_count, dtype=jnp.int32), active_orbitals])
    row_share = row_count // lax.axis_size("aux")
    aux_offset = lax.axis_index("aux") * row_share
    qmatrix = lax.psum(q_partial, "aux")
    inactive_cols = 2.0 * (inactive_fock[:, :inactive_count] + active_fock)
    active_cols = (
        jnp.dot(inactive_fock[:, inactive_count:], one_density, precision=highest) + qmatrix
    )
    fock = jnp.concatenate([inactive_cols, active_cols], axis=1)
    occ_pick = (global_rows[:, None] == occ_index[None, :]).astype(jnp.float32)
    occupied = lax.psum(jnp.dot(occ_pick.T, fock, precision=highest), "orb")
    fock_mine = lax.dynamic_slice_in_dim(fock, aux_offset, row_share, 0)
    pick_mine = lax.dynamic_slice_in_dim(occ_pick, aux_offset, row_share, 0)
    transposed = jnp.dot(pick_mine, occupied.T, precision=highest)
    return 2.0 * (fock_mine - transposed)


def solution(mesh):
    in_specs = (
        P(None, "aux", "orb"),
        P("orb", None),
        P(),
        P("aux", "orb"),
        P(),
        P("orb", None),
        P("orb", None),
    )
    out_specs = P(("orb", "aux"), None)
    return jax.shard_map(shards, mesh=mesh, in_specs=in_specs, out_specs=out_specs, check_vma=False)
```

profile of v0, /device:TPU:1, one launch (start us, length us, event | category | flops | bytes accessed | tf_op | source)
XLA Modules:
  0.0 370.7 jit_solution(4190907556177980599)
XLA Ops:
  6.5 0.0 copy-start
  6.5 0.0 all-reduce.3.cloned.1.call-start
  6.5 0.8 convert_element_type.2
  7.4 0.1 broadcast_in_dim.4
  7.5 0.1 reshape.16
  7.6 0.1 copy.22
  7.8 13.5 %fusion.7 = f32[512,56,56]{0,1,2:T(8,128)S(1)} fusion(f32[56,512,128]{2,1,0:T(8,128)} %param.7, f32[512,128]{1,0:T(8,128)S(1)} %copy.22, s32[128]{0:T(128)S(1)} %iota_add_fusion, s32[56]{0:T(128)} %param.9), kind=kOutput, calls=%fused_computation.7 | convolution fusion | flops 2469927936 | bytes 21365472 | tf_op jit(solution)/shard_map/wPp,pv->Pvw/dot_general | solution.py:24
  21.2 6.4 %copy.23 = f32[512,56,56]{0,2,1:T(8,128)} copy(f32[512,56,56]{0,1,2:T(8,128)S(1)} %fusion.7) | data formatting | bytes 12845056 | tf_op jit(solution)/shard_map/wPp,pv->Pvw/transpose | solution.py:24
  27.6 0.0 all-reduce.3.cloned.1.call-update
  27.6 0.0 copy-start.2
  27.6 0.0 copy-start.4
  27.6 0.0 copy-start.1
  27.7 0.2 all-gather.3.cloned.1.call-start
  27.9 143.9 %all-reduce.3.cloned.1.call-done = f32[512,3136]{0,1:T(8,128)} async-done(((f32[512,3136]{0,1:T(8,128)}), f32[512,3136]{0,1:T(8,128)}) %all-reduce.3.cloned.1.call-update) | async-done | bytes 6422544 | tf_op jit(solution)/shard_map/psum | solution.py:27
  171.8 0.0 copy-done
  171.8 8.6 %convolution_bitcast_fusion = f32[1,196,512]{2,1,0:T(8,128)} fusion(f32[512,3136]{0,1:T(8,128)} %all-reduce.3.cloned.1.call-done, f32[196,3136]{1,0:T(8,128)S(1)} %copy-done), kind=kOutput, calls=%fused_computation.8 | convolution fusion | flops 3776446464 | bytes 9282560 | tf_op jit(solution)/shard_map/dot_general | solution.py:28
  180.4 0.0 all-gather.3.cloned.1.call-update
  180.4 0.0 all-reduce.5.cloned.1.call-start
  180.5 0.0 copy-done.2
  180.5 0.1 copy.21
  180.6 0.0 copy-done.4
  180.6 0.1 pad_add_fusion
  180.7 0.0 copy-done.1
  180.7 63.3 %all-gather.3.cloned.1.call-done = f32[16,196,512]{2,1,0:T(8,128)} async-done(((f32[1,196,512]{2,1,0:T(8,128)}), f32[16,196,512]{2,1,0:T(8,128)}) %all-gather.3.cloned.1.call-update) | async-done | bytes 6422544 | tf_op jit(solution)/shard_map/all_gather | solution.py:29
  244.0 6.1 %reshape.20 = f32[3136,512]{1,0:T(8,128)} reshape(f32[16,196,512]{2,1,0:T(8,128)} %all-gather.3.cloned.1.call-done) | data formatting | bytes 12845056
  250.2 0.0 copy-start.3
  250.2 15.4 %fusion.11 = f32[128,56]{0,1:T(8,128)S(1)} fusion(f32[512,56,56]{0,2,1:T(8,128)} %bitcast.23, f32[56,512,128]{2,1,0:T(8,128)} %param.7, f32[512,128]{1,0:T(8,128)S(1)} %copy.22), kind=kOutput, calls=%fused_computation.11 | convolution fusion | flops 2469920768 | bytes 21393408 | tf_op jit(solution)/shard_map/uPp,Ptu->pt/dot_general | solution.py:30
  265.5 6.3 %psum.22 = f32[128,56]{0,1:T(8,128)S(1)} all-reduce(f32[128,56]{0,1:T(8,128)S(1)} %fusion.11), channel_id=1, replica_groups=mesh['orb'=16,'aux'=2] {'aux'}, use_global_device_ids=true, to_apply=%region_1.0 | all-reduce | flops 7168 | bytes 57344 | tf_op jit(solution)/shard_map/psum | solution.py:36
  271.8 0.0 copy-done.3
  271.8 0.3 convolution_add_fusion
  272.2 0.1 copy.25
  272.3 1.1 fusion.16
  273.4 0.0 all-reduce.5.cloned.1.call-update
  273.4 0.1 broadcast_compare_fusion
  273.5 88.9 %all-reduce.5.cloned.1.call-done = f32[256,256]{1,0:T(8,128)} async-done(((f32[256,256]{1,0:T(8,128)}), f32[256,256]{1,0:T(8,128)}) %all-reduce.5.cloned.1.call-update) | async-done | bytes 262160 | tf_op jit(solution)/shard_map/psum | solution.py:43
  362.3 1.9 fusion.10
  (4 shorter events, 0.0 us)
Async XLA Ops:
  6.5 165.2 %copy-start = (f32[196,3136]{1,0:T(8,128)S(1)}, f32[196,3136]{1,0:T(8,128)}, u32[]{:S(2)}) copy-start(f32[196,3136]{1,0:T(8,128)} %param.8) | copy-start | bytes 7375876
  6.5 165.2 %all-reduce.3.cloned.1.call-start = ((), (), s32[]{:S(2)}) async-start(), calls=%async_computation | async-start | bytes 12845056 | tf_op jit(solution)/shard_map/psum | solution.py:27
  27.6 152.8 %copy-start.2 = (f32[128,200]{0,1:T(8,128)S(1)}, f32[128,200]{0,1:T(8,128)}, u32[]{:S(2)}) copy-start(f32[128,200]{0,1:T(8,128)} %param.13) | copy-start | bytes 307204
  27.6 153.0 %copy-start.4 = (s32[56]{0:T(128)S(1)}, s32[56]{0:T(128)}, u32[]{:S(2)}) copy-start(s32[56]{0:T(128)} %param.9) | copy-start | bytes 676
  27.6 153.0 %copy-start.1 = (f32[128,256]{1,0:T(8,128)S(1)}, f32[128,256]{1,0:T(8,128)}, u32[]{:S(2)}) copy-start(f32[128,256]{1,0:T(8,128)} %param.12) | copy-start | bytes 393220
  27.7 216.4 %all-gather.3.cloned.1.call-start = ((), (), s32[]{:S(2)}) async-start(), calls=%async_computation.2 | async-start | bytes 6963200 | tf_op jit(solution)/shard_map/all_gather | solution.py:29
  180.4 181.9 %all-reduce.5.cloned.1.call-start = ((), (), s32[]{:S(2)}) async-start(), calls=%async_computation.1 | async-start | bytes 524288 | tf_op jit(solution)/shard_map/psum | solution.py:43
  250.2 21.7 %copy-start.3 = (f32[56,56]{1,0:T(8,128)S(1)}, f32[56,56]{1,0:T(8,128)}, u32[]{:S(2)}) copy-start(f32[56,56]{1,0:T(8,128)} %param.11) | copy-start | bytes 37636
Sparse Core Ops, SparseCore 0:
  27.7 143.9 all-reduce.2
  180.5 63.4 all-gather.2
  273.5 88.8 all-reduce.4
where the time goes:
time: 371 us
  waiting for transfers between devices  296 us (80%)
  matrix products  40.7 us (11%)
  between operations  13.2 us (4%)
  local copies, waits for them, and re-layouts  13 us (4%)
  blocking collectives  6.31 us (2%)
    psum x1, waiting for transfers between devices, shards(): pairs = lax.psum(partial_pairs, 'orb')  144 us
    psum x1, waiting for transfers between devices, shards(): occupied = lax.psum(jnp.dot(occ_pick.T, fock, precision=highest), 'orb')  88.9 us
    all_gather x1, waiting for transfers between devices, shards(): half = lax.all_gather(column_block, 'orb', axis=1, tiled=True)  63.3 us
    dot_general x1, matrix products, shards(): jnp.einsum('uPp,Ptu->pt', screened, half.reshape(slab_count, act_count, a...  15.4 us
    dot_general x1, matrix products, shards(): jnp.einsum('wPp,pv->Pvw', screened, active_pick, precision=highest)  13.5 us
    dot_general x1, matrix products, shards(): column_block = jnp.dot(pairs, pair_density.T, precision=highest)  8.61 us
  transfers between devices with their start and end apart: 3, of which 3 were waited for; matrix products, arithmetic and copies ran while one was open for 0% of the time, Pallas kernels for 0%

commit v1 on v0

--- a/solution.py
+++ b/solution.py
@@ -2,6 +2,24 @@
 import jax.numpy as jnp
 from jax import lax
 from jax.sharding import PartitionSpec as P
+
+
+def gather_around(value, axis, dim):
+    ways, here, lap = (lax.axis_size(axis), lax.axis_index(axis), value.shape[dim])
+    shape = [n * ways if d == dim else n for d, n in enumerate(value.shape)]
+    full = lax.dynamic_update_slice_in_dim(
+        jnp.zeros(shape, value.dtype), value, here * lap, axis=dim
+    )
+    going_up = going_down = value
+    for far in range(1, ways // 2 + 1):
+        going_up = lax.ppermute(going_up, axis, [(d, (d + 1) % ways) for d in range(ways)])
+        full = lax.dynamic_update_slice_in_dim(full, going_up, (here - far) % ways * lap, axis=dim)
+        if 2 * far < ways:
+            going_down = lax.ppermute(going_down, axis, [(d, (d - 1) % ways) for d in range(ways)])
+            full = lax.dynamic_update_slice_in_dim(
+                full, going_down, (here + far) % ways * lap, axis=dim
+            )
+    return full
 
 
 def shards(
@@ -26,7 +44,7 @@
     )
     pairs = lax.psum(partial_pairs, "orb")
     column_block = jnp.dot(pairs, pair_density.T, precision=highest)
-    half = lax.all_gather(column_block, "orb", axis=1, tiled=True)
+    half = gather_around(column_block, "orb", 1)
     q_partial = jnp.einsum(
         "uPp,Ptu->pt", screened, half.reshape(slab_count, act_count, act_count), precision=highest
     )

time: 371 us -> 420 us (1.13)
  local copies, waits for them, and re-layouts: 13 us -> 42.4 us
  starting transfers between devices: 0.27 us -> 19.3 us
    all_gather x1 -> x0, waiting for transfers between devices: 63.3 us -> none  [shards(): half = lax.all_gather(column_block, 'orb', axis=1, tiled=True)]
    ppermute x0 -> x15, waiting for transfers between devices: none -> 61.6 us  [the longest x8 61.1 us: gather_around(): lax.ppermute(going_up, axis, [(d, (d + 1) % ways) for d in range(ways)])]
    dynamic_update_slice x0 -> x16, local copies, waits for them, and re-layouts: none -> 31 us  [the longest x8 15.5 us: gather_around(): lax.dynamic_update_slice_in_dim(full, going_up, (here - far) % ways * lap...]
    ppermute x0 -> x15, starting transfers between devices: none -> 19.3 us  [the longest x8 19.1 us: gather_around(): lax.ppermute(going_up, axis, [(d, (d + 1) % ways) for d in range(ways)])]
    unnamed x12 -> x33, local copies, waits for them, and re-layouts: 6.23 us -> 1.06 us
  transfers between devices with their start and end apart: 3 -> 17, of which waited for: 3 -> 11; matrix products, arithmetic and copies ran while one was open for 0% -> 8% of each run, Pallas kernels for 0% -> 0%
where the time goes in v1:
time: 420 us; the launch traced here: 419 us
  waiting for transfers between devices  296 us (70%)
  local copies, waits for them, and re-layouts  42.4 us (10%)
  matrix products  39.3 us (9%)
  starting transfers between devices  19.3 us (5%)
  between operations  14 us (3%)
  blocking collectives  6.31 us (2%)
    psum x1, waiting for transfers between devices, shards(): pairs = lax.psum(partial_pairs, 'orb')  144 us
    psum x1, waiting for transfers between devices, shards(): occupied = lax.psum(jnp.dot(occ_pick.T, fock, precision=highest), 'orb')  90.4 us
    ppermute x8, waiting for transfers between devices, gather_around(): lax.ppermute(going_up, axis, [(d, (d + 1) % ways) for d in range(ways)])  61.1 us
    ppermute x8, starting transfers between devices, gather_around(): lax.ppermute(going_up, axis, [(d, (d + 1) % ways) for d in range(ways)])  19.1 us
    dynamic_update_slice x8, local copies, waits for them, and re-layouts, gather_around(): lax.dynamic_update_slice_in_dim(full, going_up, (here - far) % ways * lap...  15.5 us
    dot_general x1, matrix products, shards(): jnp.einsum('uPp,Ptu->pt', screened, half.reshape(slab_count, act_count, a...  15.4 us
    dynamic_update_slice x7, local copies, waits for them, and re-layouts, gather_around(): lax.dynamic_update_slice_in_dim(full, going_down, (here + far) % ways * l...  13.6 us
    dot_general x1, matrix products, shards(): jnp.einsum('wPp,pv->Pvw', screened, active_pick, precision=highest)  13.5 us
  transfers between devices with their start and end apart: 17, of which 11 were waited for; matrix products, arithmetic and copies ran while one was open for 8% of the time, Pallas kernels for 0%

profile of v1, /device:TPU:1, one launch (start us, length us, event | category | flops | bytes accessed | tf_op | source)
XLA Modules:
  0.0 419.3 jit_solution(9614864921741960523)
XLA Ops:
  6.5 0.8 convert_element_type.2
  7.4 0.1 broadcast_in_dim.6
  7.5 0.1 reshape.16
  7.6 0.1 copy.17
  7.8 13.5 %fusion.7 = f32[512,56,56]{0,1,2:T(8,128)S(1)} fusion(f32[56,512,128]{2,1,0:T(8,128)} %param.7, f32[512,128]{1,0:T(8,128)S(1)} %copy.17, s32[128]{0:T(128)S(1)} %iota_add_fusion, s32[56]{0:T(128)} %param.9), kind=kOutput, calls=%fused_computation.7 | convolution fusion | flops 2469927936 | bytes 21365472 | tf_op jit(solution)/shard_map/wPp,pv->Pvw/dot_general | solution.py:42
  21.2 6.4 %copy.18 = f32[512,56,56]{0,2,1:T(8,128)} copy(f32[512,56,56]{0,1,2:T(8,128)S(1)} %fusion.7) | data formatting | bytes 12845056 | tf_op jit(solution)/shard_map/wPp,pv->Pvw/transpose | solution.py:42
  27.6 0.0 all-reduce.3.cloned.1.call-update
  27.7 0.0 copy-start.14
  27.7 0.0 copy-start.15
  27.7 0.0 all-reduce.5.cloned.1.call-start
  27.7 144.1 %all-reduce.3.cloned.1.call-done = f32[512,3136]{0,1:T(8,128)} async-done(((f32[512,3136]{0,1:T(8,128)}), f32[512,3136]{0,1:T(8,128)}) %all-reduce.3.cloned.1.call-update) | async-done | bytes 6422544 | tf_op jit(solution)/shard_map/psum | solution.py:45
  171.8 7.3 %fusion.28 = f32[512,196]{0,1:T(8,128)S(1)} fusion(f32[512,3136]{0,1:T(8,128)} %all-reduce.3.cloned.1.call-done, f32[196,3136]{1,0:T(8,128)S(1)} %copy-done), kind=kOutput, calls=%fused_computation.30 | convolution fusion | flops 3776446464 | bytes 9282560 | tf_op jit(solution)/shard_map/dot_general | solution.py:46
  179.1 1.7 collective-permute-start
  180.7 9.3 %collective-permute-done = f32[512,196]{0,1:T(8,128)S(1)} collective-permute-done((f32[512,196]{0,1:T(8,128)S(1)}, f32[512,196]{0,1:T(8,128)S(1)}, u32[]{:S(2)}, u32[]{:S(2)}) %collective-permute-start) | collective-permute-done | bytes 401440 | tf_op jit(solution)/shard_map/ppermute | solution.py:15
  190.0 2.5 collective-permute-start.2
  192.5 0.1 collective-permute-start.3
  192.5 8.3 %collective-permute-done.2 = f32[512,196]{0,1:T(8,128)S(1)} collective-permute-done((f32[512,196]{0,1:T(8,128)S(1)}, f32[512,196]{0,1:T(8,128)S(1)}, u32[]{:S(2)}, u32[]{:S(2)}) %collective-permute-start.2) | collective-permute-done | bytes 401440 | tf_op jit(solution)/shard_map/ppermute | solution.py:15
  200.9 2.5 collective-permute-start.4
  203.4 0.2 collective-permute-done.3
  203.6 0.0 collective-permute-start.5
  203.6 8.4 %collective-permute-done.4 = f32[512,196]{0,1:T(8,128)S(1)} collective-permute-done((f32[512,196]{0,1:T(8,128)S(1)}, f32[512,196]{0,1:T(8,128)S(1)}, u32[]{:S(2)}, u32[]{:S(2)}) %collective-permute-start.4) | collective-permute-done | bytes 401440 | tf_op jit(solution)/shard_map/ppermute | solution.py:15
  212.0 2.5 collective-permute-start.6
  214.5 0.1 collective-permute-start.7
  214.5 12.0 %collective-permute-done.6 = f32[512,196]{0,1:T(8,128)S(1)} collective-permute-done((f32[512,196]{0,1:T(8,128)S(1)}, f32[512,196]{0,1:T(8,128)S(1)}, u32[]{:S(2)}, u32[]{:S(2)}) %collective-permute-start.6) | collective-permute-done | bytes 401440 | tf_op jit(solution)/shard_map/ppermute | solution.py:15
  226.5 2.5 collective-permute-start.8
  229.0 0.1 collective-permute-start.9
  229.1 9.2 %collective-permute-done.8 = f32[512,196]{0,1:T(8,128)S(1)} collective-permute-done((f32[512,196]{0,1:T(8,128)S(1)}, f32[512,196]{0,1:T(8,128)S(1)}, u32[]{:S(2)}, u32[]{:S(2)}) %collective-permute-start.8) | collective-permute-done | bytes 401440 | tf_op jit(solution)/shard_map/ppermute | solution.py:15
  238.3 2.5 collective-permute-start.10
  240.8 0.0 collective-permute-done.9
  240.8 0.0 collective-permute-start.11
  240.8 9.2 %collective-permute-done.10 = f32[512,196]{0,1:T(8,128)S(1)} collective-permute-done((f32[512,196]{0,1:T(8,128)S(1)}, f32[512,196]{0,1:T(8,128)S(1)}, u32[]{:S(2)}, u32[]{:S(2)}) %collective-permute-start.10) | collective-permute-done | bytes 401440 | tf_op jit(solution)/shard_map/ppermute | solution.py:15
  250.1 2.5 collective-permute-start.12
  252.5 0.2 collective-permute-done.11
  252.7 4.7 %collective-permute-done.12 = f32[512,196]{0,1:T(8,128)} collective-permute-done((f32[512,196]{0,1:T(8,128)S(1)}, f32[512,196]{0,1:T(8,128)}, u32[]{:S(2)}, u32[]{:S(2)}) %collective-permute-start.12) | collective-permute-done | bytes 401440 | tf_op jit(solution)/shard_map/ppermute | solution.py:15
  257.4 2.6 collective-permute-start.14
  260.0 0.3 fusion.19
  260.6 1.0 copy.16
  261.8 0.1 pad_add_fusion
  261.8 0.9 add_multiply_fusion
  262.8 3.5 broadcast_in_dim.15
  266.3 1.8 dynamic_update_slice.48
  268.1 2.0 dynamic_update_slice.49
  270.1 1.9 dynamic_update_slice.50
  272.0 1.9 dynamic_update_slice.51
  273.9 1.9 dynamic_update_slice.52
  275.9 1.9 dynamic_update_slice.53
  277.8 2.0 dynamic_update_slice.54
  279.8 2.0 dynamic_update_slice.55
  281.7 2.0 dynamic_update_slice.56
  283.7 1.9 dynamic_update_slice.57
  285.6 2.0 dynamic_update_slice.58
  287.5 1.9 dynamic_update_slice.59
  289.5 1.9 dynamic_update_slice.60
  291.4 1.9 dynamic_update_slice.61
  293.3 2.0 dynamic_update_slice.62
  295.3 2.0 dynamic_update_slice.63
  297.3 15.4 %fusion.11 = f32[128,56]{0,1:T(8,128)S(1)} fusion(f32[512,56,56]{0,2,1:T(8,128)} %bitcast.17, f32[56,512,128]{2,1,0:T(8,128)} %param.7, f32[512,128]{1,0:T(8,128)S(1)} %copy.17), kind=kOutput, calls=%fused_computation.10 | convolution fusion | flops 2469920768 | bytes 21393408 | tf_op jit(solution)/shard_map/uPp,Ptu->pt/dot_general | solution.py:48
  312.6 6.3 %psum.22 = f32[128,56]{0,1:T(8,128)S(1)} all-reduce(f32[128,56]{0,1:T(8,128)S(1)} %fusion.11), channel_id=1, replica_groups=mesh['orb'=16,'aux'=2] {'aux'}, use_global_device_ids=true, to_apply=%region_1.2 | all-reduce | flops 7168 | bytes 57344 | tf_op jit(solution)/shard_map/psum | solution.py:54
  319.0 0.1 copy.20
  319.1 1.1 fusion.16
  320.1 0.0 all-reduce.5.cloned.1.call-update
  320.2 0.1 broadcast_compare_fusion
  320.3 90.4 %all-reduce.5.cloned.1.call-done = f32[256,256]{1,0:T(8,128)} async-done(((f32[256,256]{1,0:T(8,128)}), f32[256,256]{1,0:T(8,128)}) %all-reduce.5.cloned.1.call-update) | async-done | bytes 262160 | tf_op jit(solution)/shard_map/psum | solution.py:61
  410.6 1.9 fusion.10
  (42 shorter events, 0.1 us)
Async XLA Ops:
  6.5 165.3 %copy-start = (f32[196,3136]{1,0:T(8,128)S(1)}, f32[196,3136]{1,0:T(8,128)}, u32[]{:S(2)}) copy-start(f32[196,3136]{1,0:T(8,128)} %param.8) | copy-start | bytes 7375876
  6.5 165.3 %all-reduce.3.cloned.1.call-start = ((), (), s32[]{:S(2)}) async-start(), calls=%async_computation | async-start | bytes 12845056 | tf_op jit(solution)/shard_map/psum | solution.py:45
  27.6 232.4 %copy-start.13 = (f32[128,256]{1,0:T(8,128)S(1)}, f32[128,256]{1,0:T(8,128)}, u32[]{:S(2)}) copy-start(f32[128,256]{1,0:T(8,128)} %param.12) | copy-start | bytes 393220
  27.7 232.4 %copy-start.14 = (f32[56,56]{1,0:T(8,128)S(1)}, f32[56,56]{1,0:T(8,128)}, u32[]{:S(2)}) copy-start(f32[56,56]{1,0:T(8,128)} %param.11) | copy-start | bytes 37636
  27.7 234.1 %copy-start.15 = (s32[56]{0:T(128)S(1)}, s32[56]{0:T(128)}, u32[]{:S(2)}) copy-start(s32[56]{0:T(128)} %param.9) | copy-start | bytes 676
  27.7 382.9 %all-reduce.5.cloned.1.call-start = ((), (), s32[]{:S(2)}) async-start(), calls=%async_computation.1 | async-start | bytes 524288 | tf_op jit(solution)/shard_map/psum | solution.py:61
  179.1 10.9 %collective-permute-start = (f32[512,196]{0,1:T(8,128)S(1)}, f32[512,196]{0,1:T(8,128)S(1)}, u32[]{:S(2)}, u32[]{:S(2)}) collective-permute-start(f32[512,196]{0,1:T(8,128)S(1)} %fusion.28), channel_id=1, source_target_pairs={{0,2},{2,4},{4,6},{6,8},{8,10},{10,12},{12,14},{14,16},{16,18},{18... | collective-permute-start | bytes 1204232 | tf_op jit(solution)/shard_map/ppermute | solution.py:15
  180.7 11.8 %collective-permute-start.1 = (f32[512,196]{0,1:T(8,128)S(1)}, f32[512,196]{0,1:T(8,128)S(1)}, u32[]{:S(2)}, u32[]{:S(2)}) collective-permute-start(f32[512,196]{0,1:T(8,128)S(1)} %fusion.28), channel_id=1, source_target_pairs={{0,30},{2,0},{4,2},{6,4},{8,6},{10,8},{12,10},{14,12},{16,14},{18,... | collective-permute-start | bytes 1204232 | tf_op jit(solution)/shard_map/ppermute | solution.py:18
  190.0 2.5 copy-start.1
  190.0 10.9 %collective-permute-start.2 = (f32[512,196]{0,1:T(8,128)S(1)}, f32[512,196]{0,1:T(8,128)S(1)}, u32[]{:S(2)}, u32[]{:S(2)}) collective-permute-start(f32[512,196]{0,1:T(8,128)S(1)} %collective-permute-done), channel_id=1, source_target_pairs={{0,2},{2,4},{4,6},{6,8},{8,10},{10,12},{12,14},{14,16},{16,18},{18... | collective-permute-start | bytes 1204232 | tf_op jit(solution)/shard_map/ppermute | solution.py:15
  192.5 8.4 %copy-start.2 = (f32[512,196]{0,1:T(8,128)}, f32[512,196]{0,1:T(8,128)S(1)}, u32[]{:S(2)}) copy-start(f32[512,196]{0,1:T(8,128)S(1)} %collective-permute-done.1) | copy-start | bytes 1204228
  192.5 11.1 %collective-permute-start.3 = (f32[512,196]{0,1:T(8,128)S(1)}, f32[512,196]{0,1:T(8,128)S(1)}, u32[]{:S(2)}, u32[]{:S(2)}) collective-permute-start(f32[512,196]{0,1:T(8,128)S(1)} %collective-permute-done.1), channel_id=1, source_target_pairs={{0,30},{2,0},{4,2},{6,4},{8,6},{10,8},{12,10},{14,12},{16,14},{18,... | collective-permute-start | bytes 1204232 | tf_op jit(solution)/shard_map/ppermute | solution.py:18
  200.9 2.7 copy-start.3
  200.9 11.1 %collective-permute-start.4 = (f32[512,196]{0,1:T(8,128)S(1)}, f32[512,196]{0,1:T(8,128)S(1)}, u32[]{:S(2)}, u32[]{:S(2)}) collective-permute-start(f32[512,196]{0,1:T(8,128)S(1)} %collective-permute-done.2), channel_id=1, source_target_pairs={{0,2},{2,4},{4,6},{6,8},{8,10},{10,12},{12,14},{14,16},{16,18},{18... | collective-permute-start | bytes 1204232 | tf_op jit(solution)/shard_map/ppermute | solution.py:15
  203.6 8.4 %copy-start.4 = (f32[512,196]{0,1:T(8,128)}, f32[512,196]{0,1:T(8,128)S(1)}, u32[]{:S(2)}) copy-start(f32[512,196]{0,1:T(8,128)S(1)} %collective-permute-done.3) | copy-start | bytes 1204228
  203.6 10.9 %collective-permute-start.5 = (f32[512,196]{0,1:T(8,128)S(1)}, f32[512,196]{0,1:T(8,128)S(1)}, u32[]{:S(2)}, u32[]{:S(2)}) collective-permute-start(f32[512,196]{0,1:T(8,128)S(1)} %collective-permute-done.3), channel_id=1, source_target_pairs={{0,30},{2,0},{4,2},{6,4},{8,6},{10,8},{12,10},{14,12},{16,14},{18,... | collective-permute-start | bytes 1204232 | tf_op jit(solution)/shard_map/ppermute | solution.py:18
  212.0 2.5 copy-start.5
  212.0 14.5 %collective-permute-start.6 = (f32[512,196]{0,1:T(8,128)S(1)}, f32[512,196]{0,1:T(8,128)S(1)}, u32[]{:S(2)}, u32[]{:S(2)}) collective-permute-start(f32[512,196]{0,1:T(8,128)S(1)} %collective-permute-done.4), channel_id=1, source_target_pairs={{0,2},{2,4},{4,6},{6,8},{8,10},{10,12},{12,14},{14,16},{16,18},{18... | collective-permute-start | bytes 1204232 | tf_op jit(solution)/shard_map/ppermute | solution.py:15
  214.5 12.0 %copy-start.6 = (f32[512,196]{0,1:T(8,128)}, f32[512,196]{0,1:T(8,128)S(1)}, u32[]{:S(2)}) copy-start(f32[512,196]{0,1:T(8,128)S(1)} %collective-permute-done.5) | copy-start | bytes 1204228
  214.5 14.5 %collective-permute-start.7 = (f32[512,196]{0,1:T(8,128)S(1)}, f32[512,196]{0,1:T(8,128)S(1)}, u32[]{:S(2)}, u32[]{:S(2)}) collective-permute-start(f32[512,196]{0,1:T(8,128)S(1)} %collective-permute-done.5), channel_id=1, source_target_pairs={{0,30},{2,0},{4,2},{6,4},{8,6},{10,8},{12,10},{14,12},{16,14},{18,... | collective-permute-start | bytes 1204232 | tf_op jit(solution)/shard_map/ppermute | solution.py:18
  226.5 2.5 copy-start.7
  226.5 11.8 %collective-permute-start.8 = (f32[512,196]{0,1:T(8,128)S(1)}, f32[512,196]{0,1:T(8,128)S(1)}, u32[]{:S(2)}, u32[]{:S(2)}) collective-permute-start(f32[512,196]{0,1:T(8,128)S(1)} %collective-permute-done.6), channel_id=1, source_target_pairs={{0,2},{2,4},{4,6},{6,8},{8,10},{10,12},{12,14},{14,16},{16,18},{18... | collective-permute-start | bytes 1204232 | tf_op jit(solution)/shard_map/ppermute | solution.py:15
  229.0 9.3 %copy-start.8 = (f32[512,196]{0,1:T(8,128)}, f32[512,196]{0,1:T(8,128)S(1)}, u32[]{:S(2)}) copy-start(f32[512,196]{0,1:T(8,128)S(1)} %collective-permute-done.7) | copy-start | bytes 1204228
  229.0 11.8 %collective-permute-start.9 = (f32[512,196]{0,1:T(8,128)S(1)}, f32[512,196]{0,1:T(8,128)S(1)}, u32[]{:S(2)}, u32[]{:S(2)}) collective-permute-start(f32[512,196]{0,1:T(8,128)S(1)} %collective-permute-done.7), channel_id=1, source_target_pairs={{0,30},{2,0},{4,2},{6,4},{8,6},{10,8},{12,10},{14,12},{16,14},{18,... | collective-permute-start | bytes 1204232 | tf_op jit(solution)/shard_map/ppermute | solution.py:18
  238.3 2.5 copy-start.9
  238.3 11.8 %collective-permute-start.10 = (f32[512,196]{0,1:T(8,128)S(1)}, f32[512,196]{0,1:T(8,128)S(1)}, u32[]{:S(2)}, u32[]{:S(2)}) collective-permute-start(f32[512,196]{0,1:T(8,128)S(1)} %collective-permute-done.8), channel_id=1, source_target_pairs={{0,2},{2,4},{4,6},{6,8},{8,10},{10,12},{12,14},{14,16},{16,18},{18... | collective-permute-start | bytes 1204232 | tf_op jit(solution)/shard_map/ppermute | solution.py:15
  240.8 9.2 %copy-start.11 = (f32[512,196]{0,1:T(8,128)}, f32[512,196]{0,1:T(8,128)S(1)}, u32[]{:S(2)}) copy-start(f32[512,196]{0,1:T(8,128)S(1)} %collective-permute-done.9) | copy-start | bytes 1204228
  240.8 11.9 %collective-permute-start.11 = (f32[512,196]{0,1:T(8,128)S(1)}, f32[512,196]{0,1:T(8,128)}, u32[]{:S(2)}, u32[]{:S(2)}) collective-permute-start(f32[512,196]{0,1:T(8,128)S(1)} %collective-permute-done.9), channel_id=1, source_target_pairs={{0,30},{2,0},{4,2},{6,4},{8,6},{10,8},{12,10},{14,12},{16,14},{18,... | collective-permute-start | bytes 1204232 | tf_op jit(solution)/shard_map/ppermute | solution.py:18
  250.1 2.6 copy-start.12
  250.1 7.4 %collective-permute-start.12 = (f32[512,196]{0,1:T(8,128)S(1)}, f32[512,196]{0,1:T(8,128)}, u32[]{:S(2)}, u32[]{:S(2)}) collective-permute-start(f32[512,196]{0,1:T(8,128)S(1)} %collective-permute-done.10), channel_id=1, source_target_pairs={{0,2},{2,4},{4,6},{6,8},{8,10},{10,12},{12,14},{14,16},{16,18},{18... | collective-permute-start | bytes 1204232 | tf_op jit(solution)/shard_map/ppermute | solution.py:15
  252.7 40.6 %collective-permute-start.13 = (f32[512,196]{0,1:T(8,128)}, f32[512,196]{0,1:T(8,128)}, u32[]{:S(2)}, u32[]{:S(2)}) collective-permute-start(f32[512,196]{0,1:T(8,128)} %collective-permute-done.11), channel_id=1, source_target_pairs={{0,30},{2,0},{4,2},{6,4},{8,6},{10,8},{12,10},{14,12},{16,14},{18,... | collective-permute-start | bytes 1204232 | tf_op jit(solution)/shard_map/ppermute | solution.py:18
  257.4 37.9 %collective-permute-start.14 = (f32[512,196]{0,1:T(8,128)}, f32[512,196]{0,1:T(8,128)}, u32[]{:S(2)}, u32[]{:S(2)}) collective-permute-start(f32[512,196]{0,1:T(8,128)} %collective-permute-done.12), channel_id=1, source_target_pairs={{0,2},{2,4},{4,6},{6,8},{8,10},{10,12},{12,14},{14,16},{16,18},{18... | collective-permute-start | bytes 1204232 | tf_op jit(solution)/shard_map/ppermute | solution.py:15
  268.1 15.6 %copy-start.10 = (f32[512,196]{0,1:T(8,128)S(1)}, f32[512,196]{0,1:T(8,128)}, u32[]{:S(2)}) copy-start(f32[512,196]{0,1:T(8,128)} %copy-done.9) | copy-start | bytes 1204228
Sparse Core Ops, SparseCore 0:
  27.8 143.9 all-reduce.2
  320.3 90.2 all-reduce.4
